TPU v7x, 32 devices: a whole 2x2x4 slice. The times are simulated.
32 devices in a mesh: site: 8 (over y, x, core), dp: 4 (over z).
Axes of the slice: x: 2, y: 2, z: 4, core: 2. Of those that a mesh axis runs over, the one named last changes fastest.
Arguments:
- inputs: bfloat16 [8, 12, 32, 4096], P('dp', None, None, 'site'), may hold values from -6 to 6
- cot_out: bfloat16 [8, 12, 32, 4096], P('dp', None, None, 'site'), may hold values from -18 to 18
- cot_skip: bfloat16 [8, 12, 256, 4096], P('dp', None, None, 'site'), may hold values from -6 to 6
- w_conv: bfloat16 [64, 64], replicated, may hold values from -0.75 to 0.75
- convolution_bias: float32 [64], replicated, may hold values from -3 to 3
- w_mix: bfloat16 [32, 96], replicated, may hold values from -0.625 to 0.625
- w_skip: bfloat16 [256, 32], replicated, may hold values from -1 to 1
- adj_cols: int32 [32, 4], P('site'), may hold values from 0 to 5, as said below
- used_block_count: int32 [32], P('site'), may hold values from 1 to 4, as said below
- adj_vals: bfloat16 [32, 4, 128, 128], P('site'), may hold values from -0.375 to 0.375
Outputs:
- grad_conv: float32 [64, 64], replicated
- grad_bias: float32 [64], replicated
- grad_mix: float32 [32, 96], replicated
- skip_weight_gradient: float32 [256, 32], replicated
- grad_inputs: bfloat16 [8, 12, 32, 4096], P('dp', None, None, 'site')
Inputs may be any that keep to these rules, and one draw needn't show every extreme that they name: `adj_cols`: the 4 entries of a row are different column blocks of the partition's window. The first used_block_count entries of a row of adj_cols are used; every partition has a row block using all 4.
All inputs are finite; a program needn't handle non-finite values.
Results may differ from a plain program's by a relative error of at most 0.0057.
Values may be sent and summed in bfloat16 or wider, within the bound.
A program may use at most 64 MiB of HBM per device.

v0:
```python
import jax
import jax.numpy as jnp
from jax import lax
from jax.sharding import PartitionSpec as P

BLK = 128


def with_halo(x, sides, width):
    for axis, dim in sides:
        devices, length = (lax.axis_size(axis), x.shape[dim])
        up = [(i, (i + 1) % devices) for i in range(devices)]
        down = [(j, i) for i, j in up]
        last = lax.slice_in_dim(x, length - width, length, axis=dim)
        first = lax.slice_in_dim(x, 0, width, axis=dim)
        before = lax.ppermute(last, axis, up)
        after = lax.ppermute(first, axis, down)
        x = jnp.concatenate([before, x, after], axis=dim)
    return x


def block_matrix(adj_cols, used_block_count, adj_vals):
    row_count, block_level_depth = adj_cols.shape
    blk_size = adj_vals.shape[-1]
    window_blocks = row_count + 2
    selected_blocks = (
        adj_cols[:, :, None] == jnp.arange(window_blocks, dtype=jnp.int32)[None, None, :]
    )
    alive_flags = (
        jnp.arange(block_level_depth, dtype=jnp.int32)[None, :] < used_block_count[:, None]
    )
    selection_mask = (selected_blocks & alive_flags[:, :, None]).astype(jnp.float32)
    blockwise = jnp.einsum("nkc,nkji->cjni", selection_mask, adj_vals.astype(jnp.float32))
    return blockwise.reshape(window_blocks * blk_size, row_count * blk_size).astype(jnp.bfloat16)


def apply_hop(field, matrix):
    extended = with_halo(field, (("site", 1),), BLK)
    return jnp.dot(extended, matrix, preferred_element_type=jnp.float32).astype(jnp.bfloat16)


def both_hops(hidden_rows, matrix):
    first_hop = apply_hop(hidden_rows, matrix)
    second_hop = apply_hop(first_hop, matrix)
    return (first_hop, second_hop)


def hop_backward(grad_field, matrix):
    contrib = lax.dot_general(
        grad_field, matrix, (((1,), (1,)), ((), ())), preferred_element_type=jnp.float32
    )
    middle = contrib[:, BLK:-BLK]
    boundary = jnp.concatenate([contrib[:, :BLK], contrib[:, -BLK:]], axis=1)
    received = with_halo(boundary, (("site", 1),), BLK)
    middle = middle.at[:, :BLK].add(received[:, :BLK])
    middle = middle.at[:, -BLK:].add(received[:, -BLK:])
    return middle


def shards(
    inputs,
    cot_out,
    cot_skip,
    w_conv,
    convolution_bias,
    w_mix,
    w_skip,
    adj_cols,
    used_block_count,
    adj_vals,
):
    n_batch, step_count, channel_count, site_count = inputs.shape
    matrix = block_matrix(adj_cols, used_block_count, adj_vals)
    earlier = jnp.pad(inputs[:, :-1], ((0, 0), (1, 0), (0, 0), (0, 0)))
    stacked_blocks = jnp.concatenate([earlier, inputs], axis=2)
    preactivation = (
        jnp.einsum("oc,btcs->btos", w_conv, stacked_blocks, preferred_element_type=jnp.float32)
        + convolution_bias[None, None, :, None]
    )
    filt = jnp.tanh(preactivation[:, :, :channel_count])
    gate = jax.nn.sigmoid(preactivation[:, :, channel_count:])
    hidden_state = (filt * gate).astype(jnp.bfloat16)
    n_rows = n_batch * step_count * channel_count
    first_hop, second_hop = both_hops(hidden_state.reshape(n_rows, site_count), matrix)
    four_d = (n_batch, step_count, channel_count, site_count)
    mixed_in = jnp.concatenate(
        [hidden_state, first_hop.reshape(four_d), second_hop.reshape(four_d)], axis=2
    )
    grad_mix = jnp.einsum("btos,btjs->oj", cot_out, mixed_in, preferred_element_type=jnp.float32)
    skip_weight_gradient = jnp.einsum(
        "btks,btcs->kc", cot_skip, hidden_state, preferred_element_type=jnp.float32
    )
    mixing_backward = jnp.einsum(
        "oj,btos->btjs", w_mix, cot_out, preferred_element_type=jnp.float32
    )
    grad_second = (
        mixing_backward[:, :, 2 * channel_count :].astype(jnp.bfloat16).reshape(n_rows, site_count)
    )
    first_hop_gradient = (
        mixing_backward[:, :, channel_count : 2 * channel_count].reshape(n_rows, site_count)
        + hop_backward(grad_second, matrix)
    ).astype(jnp.bfloat16)
    skip_back = jnp.einsum("kc,btks->btcs", w_skip, cot_skip, preferred_element_type=jnp.float32)
    hidden_gradient = (
        mixing_backward[:, :, :channel_count]
        + hop_backward(first_hop_gradient, matrix).reshape(four_d)
        + skip_back
    )
    grad_pre = jnp.concatenate(
        [
            hidden_gradient * gate * (1.0 - filt * filt),
            hidden_gradient * filt * gate * (1.0 - gate),
        ],
        axis=2,
    ).astype(jnp.bfloat16)
    grad_conv = jnp.einsum(
        "btos,btis->oi", grad_pre, stacked_blocks, preferred_element_type=jnp.float32
    )
    grad_bias = jnp.sum(grad_pre.astype(jnp.float32), axis=(0, 1, 3))
    back_in = jnp.einsum("oi,btos->btis", w_conv, grad_pre, preferred_element_type=jnp.float32)
    grad_inputs = back_in[:, :, channel_count:] + jnp.pad(
        back_in[:, 1:, :channel_count], ((0, 0), (0, 1), (0, 0), (0, 0))
    )
    grad_conv, grad_bias, grad_mix, skip_weight_gradient = lax.psum(
        (grad_conv, grad_bias, grad_mix, skip_weight_gradient), ("site", "dp")
    )
    return (grad_conv, grad_bias, grad_mix, skip_weight_gradient, grad_inputs.astype(jnp.bfloat16))


def solution(mesh):
    placed = (
        P("dp", None, None, "site"),
        P("dp", None, None, "site"),
        P("dp", None, None, "site"),
        P(),
        P(),
        P(),
        P(),
        P("site", None),
        P("site"),
        P("site", None, None, None),
    )
    return jax.shard_map(
        shards,
        mesh=mesh,
        in_specs=placed,
        out_specs=(P(), P(), P(), P(), P("dp", None, None, "site")),
        check_vma=False,
    )
```

profile of v0, /device:TPU:0, one launch (start us, length us, event | category | flops | bytes accessed | tf_op | source)
XLA Modules:
  0.0 95.7 jit_solution(10782161273987552306)
XLA Ops:
  0.6 0.0 copy-start
  0.6 0.8 iota_compare_fusion.2
  1.4 1.7 %fusion.14 = bf16[6,128,4,128]{3,0,1,2:T(8,128)(2,1)S(1)} fusion(bf16[4,4,128,128]{3,2,1,0:T(8,128)(2,1)} %param.27, s32[4,4]{1,0:T(4,128)} %param.25, pred[4,4]{1,0:T(4,128)(4,1)S(1)} %iota_compare_fusion.2), kind=kOutput, calls=%fused_computation.32 | convolution fusion | flops 3539136 | bytes 1310800 | tf_op jit(solution)/shard_map/nkc,nkji->cjni/dot_general | solution.py:33
  3.2 0.6 copy.18
  3.8 0.8 convolution_bitcast_fusion
  4.7 0.1 slice.215
  4.8 0.8 fusion.32
  5.6 0.1 fusion.66
  5.7 0.5 collective-permute-start
  6.2 2.9 %collective-permute-start.1 = (f32[768,128]{1,0:T(8,128)S(1)}, f32[768,128]{1,0:T(8,128)S(1)}, u32[]{:S(2)}, u32[]{:S(2)}) collective-permute-start(f32[768,128]{1,0:T(8,128)S(1)} %get-tuple-element.62), channel_id=1, source_target_pairs={{4,0},{8,4},{12,8},{16,12},{20,16},{24,20},{28,24},{0,28},{5,1},{9... | collective-permute-start | bytes 1179656 | tf_op jit(solution)/shard_map/ppermute | solution.py:17
  9.1 0.2 slice.158
  9.4 0.6 compare_reduce_fusion
  10.0 6.1 %collective-permute-done = f32[768,128]{1,0:T(8,128)S(1)} collective-permute-done((f32[768,128]{1,0:T(8,128)S(1)}, f32[768,128]{1,0:T(8,128)S(1)}, u32[]{:S(2)}, u32[]{:S(2)}) %collective-permute-start) | collective-permute-done | bytes 393248 | tf_op jit(solution)/shard_map/ppermute | solution.py:16
  16.1 0.9 fusion.41
  16.9 0.7 collective-permute-done.1
  17.6 0.1 fusion.44
  17.7 0.0 slice-start.1
  17.7 0.4 fusion.13
  18.1 0.8 fusion.30
  18.9 0.1 fusion.65
  19.0 0.0 copy-start.2
  19.0 1.8 %collective-permute-start.2 = (f32[768,128]{1,0:T(8,128)S(1)}, f32[768,128]{1,0:T(8,128)S(1)}, u32[]{:S(2)}, u32[]{:S(2)}) collective-permute-start(f32[768,128]{1,0:T(8,128)S(1)} %get-tuple-element.61), channel_id=1, source_target_pairs={{0,4},{4,8},{8,12},{12,16},{16,20},{20,24},{24,28},{28,0},{1,5},{5... | collective-permute-start | bytes 1179656 | tf_op jit(solution)/shard_map/ppermute | solution.py:16
  20.9 1.2 %fusion.47 = f32[2,12,512,32]{2,3,1,0:T(8,128)S(1)} fusion(bf16[2,12,256,512]{3,2,1,0:T(8,128)(2,1)S(1)} %bitcast.81, bf16[256,32]{0,1:T(8,128)(2,1)S(1)} %copy-done.3), kind=kOutput, calls=%fused_computation.67 | convolution fusion | flops 201326592 | bytes 7880704 | tf_op jit(solution)/shard_map/kc,btks->btcs/dot_general | solution.py:103
  22.0 0.0 slice-start.2
  22.1 0.1 slice.146
  22.1 1.7 %collective-permute-start.3 = (f32[768,128]{1,0:T(8,128)S(1)}, f32[768,128]{1,0:T(8,128)S(1)}, u32[]{:S(2)}, u32[]{:S(2)}) collective-permute-start(f32[768,128]{1,0:T(8,128)S(1)} %get-tuple-element.60), channel_id=1, source_target_pairs={{4,0},{8,4},{12,8},{16,12},{20,16},{24,20},{28,24},{0,28},{5,1},{9... | collective-permute-start | bytes 1179656 | tf_op jit(solution)/shard_map/ppermute | solution.py:17
  23.9 0.5 add_bitcast_fusion
  24.4 0.2 slice.163
  24.6 3.8 %collective-permute-done.2 = f32[768,128]{1,0:T(8,128)S(1)} collective-permute-done((f32[768,128]{1,0:T(8,128)S(1)}, f32[768,128]{1,0:T(8,128)S(1)}, u32[]{:S(2)}, u32[]{:S(2)}) %collective-permute-start.2) | collective-permute-done | bytes 393248 | tf_op jit(solution)/shard_map/ppermute | solution.py:16
  28.4 0.7 fusion.42
  29.1 1.2 %collective-permute-done.3 = f32[768,128]{1,0:T(8,128)S(1)} collective-permute-done((f32[768,128]{1,0:T(8,128)S(1)}, f32[768,128]{1,0:T(8,128)S(1)}, u32[]{:S(2)}, u32[]{:S(2)}) %collective-permute-start.3) | collective-permute-done | bytes 393248 | tf_op jit(solution)/shard_map/ppermute | solution.py:17
  30.4 0.1 fusion.43
  30.5 1.2 %multiply_convert_fusion.2 = (bf16[2,12,32,512]{3,2,1,0:T(8,128)(2,1)S(1)}, bf16[2,12,32,512]{3,2,1,0:T(8,128)(2,1)S(1)}, bf16[2,12,32,512]{3,2,1,0:T(8,128)(2,1)S(1)}) fusion(f32[2,12,64,512]{3,2,1,0:T(8,128)S(1)} %add_bitcast_fusion, f32[2,12,512,32]{2,3,1,0:T(8,128)S(1)} %fusion.47, f32[2,12,32,512]{3,2,1,0:T(8,128)S(1)} %bitcast.84, ...), kind=kLoop, calls=%fused_computation.28 | loop fusion | flops 6684672 | bytes 10223616 | tf_op jit(solution)/shard_map/convert
  31.7 0.6 convolution_bitcast_fusion.1
  32.4 0.3 convert_reduce_fusion
  32.7 0.1 slice.175
  32.9 1.9 %convolution_bitcast_fusion.2 = f32[256,32]{0,1:T(8,128)S(1)} fusion(bf16[2,12,32,512]{3,2,1,0:T(8,128)(2,1)S(1)} %get-tuple-element.59, bf16[2,12,256,512]{3,2,1,0:T(8,128)(2,1)S(1)} %bitcast.81), kind=kOutput, calls=%fused_computation.43 | convolution fusion | flops 201326592 | bytes 7110656 | tf_op jit(solution)/shard_map/btks,btcs->kc/dot_general | solution.py:90
  34.8 2.9 %collective-permute-start.4 = (bf16[768,128]{1,0:T(8,128)(2,1)S(1)}, bf16[768,128]{1,0:T(8,128)(2,1)S(1)}, u32[]{:S(2)}, u32[]{:S(2)}) collective-permute-start(bf16[768,128]{1,0:T(8,128)(2,1)S(1)} %get-tuple-element.66), channel_id=1, source_target_pairs={{0,4},{4,8},{8,12},{12,16},{16,20},{20,24},{24,28},{28,0},{1,5},{5... | collective-permute-start | bytes 589832 | tf_op jit(solution)/shard_map/ppermute | solution.py:16
  37.8 1.1 %fusion.8 = bf16[2,12,32,512]{3,2,1,0:T(8,128)(2,1)} fusion(f32[2,12,64,512]{3,2,1,0:T(8,128)S(1)} %convolution_bitcast_fusion.1, f32[2,11,32,512]{3,2,1,0:T(8,128)S(1)} %slice.175), kind=kLoop, calls=%fused_computation.14 | loop fusion | flops 786432 | bytes 3801088 | tf_op jit(solution)/shard_map/convert_element_type | solution.py:127
  38.9 3.6 %collective-permute-done.4 = bf16[768,128]{1,0:T(8,128)(2,1)S(1)} collective-permute-done((bf16[768,128]{1,0:T(8,128)(2,1)S(1)}, bf16[768,128]{1,0:T(8,128)(2,1)S(1)}, u32[]{:S(2)}, u32[]{:S(2)}) %collective-permute-start.4) | collective-permute-done | bytes 196640 | tf_op jit(solution)/shard_map/ppermute | solution.py:16
  42.5 0.8 convolution_convert_fusion.2
  43.3 2.1 %collective-permute-start.6 = (bf16[768,128]{1,0:T(8,128)(2,1)S(1)}, bf16[768,128]{1,0:T(8,128)(2,1)S(1)}, u32[]{:S(2)}, u32[]{:S(2)}) collective-permute-start(bf16[768,128]{1,0:T(8,128)(2,1)S(1)} %get-tuple-element.64), channel_id=1, source_target_pairs={{0,4},{4,8},{8,12},{12,16},{16,20},{20,24},{24,28},{28,0},{1,5},{5... | collective-permute-start | bytes 589832 | tf_op jit(solution)/shard_map/ppermute | solution.py:16
  45.5 0.6 collective-permute-start.7
  46.1 0.5 convolution_bitcast_fusion.3
  46.7 4.2 %collective-permute-done.6 = bf16[768,128]{1,0:T(8,128)(2,1)S(1)} collective-permute-done((bf16[768,128]{1,0:T(8,128)(2,1)S(1)}, bf16[768,128]{1,0:T(8,128)(2,1)S(1)}, u32[]{:S(2)}, u32[]{:S(2)}) %collective-permute-start.6) | collective-permute-done | bytes 196640 | tf_op jit(solution)/shard_map/ppermute | solution.py:16
  50.9 0.8 convolution_convert_fusion.1
  51.6 0.9 fusion.25
  52.5 43.2 %all-reduce.2 = (f32[64,64]{1,0:T(8,128)}, f32[64]{0:T(128)}, f32[32,96]{1,0:T(8,128)}, f32[256,32]{0,1:T(8,128)}) all-reduce(f32[64,64]{1,0:T(8,128)S(1)} %convolution_bitcast_fusion.3, f32[64]{0:T(128)S(1)} %convert_reduce_fusion, f32[32,96]{1,0:T(8,128)S(1)} %fusion.25, ...), channel_id=1, replica_groups=mesh['site'=8,'dp'=4] {'site','dp'}, use_global_device_ids=true, to_apply=%region_1.2 | all-reduce | flops 15424 | bytes 123392 | tf_op jit(solution)/shard_map/psum | solution.py:124
  (27 shorter events, 0.1 us)
Async XLA Ops:
  0.6 3.2 %copy-start = (bf16[2,12,32,512]{3,2,1,0:T(8,128)(2,1)S(1)}, bf16[2,12,32,512]{3,2,1,0:T(8,128)(2,1)}, u32[]{:S(2)}) copy-start(bf16[2,12,32,512]{3,2,1,0:T(8,128)(2,1)} %param.19) | copy-start | bytes 2359300
  1.4 2.4 %copy-start.5 = (bf16[32,96]{1,0:T(8,128)(2,1)S(1)}, bf16[32,96]{1,0:T(8,128)(2,1)}, u32[]{:S(2)}) copy-start(bf16[32,96]{1,0:T(8,128)(2,1)} %param.23) | copy-start | bytes 18436
  4.6 4.7 %copy-start.1 = (f32[2,12,96,512]{3,2,1,0:T(8,128)}, f32[2,12,96,512]{3,2,1,0:T(8,128)S(1)}, u32[]{:S(2)}) copy-start(f32[2,12,96,512]{3,2,1,0:T(8,128)S(1)} %convolution_bitcast_fusion) | copy-start | bytes 14155780
  5.7 10.4 %collective-permute-start = (f32[768,128]{1,0:T(8,128)S(1)}, f32[768,128]{1,0:T(8,128)S(1)}, u32[]{:S(2)}, u32[]{:S(2)}) collective-permute-start(f32[768,128]{1,0:T(8,128)S(1)} %get-tuple-element.63), channel_id=1, source_target_pairs={{0,4},{4,8},{8,12},{12,16},{16,20},{20,24},{24,28},{28,0},{1,5},{5... | collective-permute-start | bytes 1179656 | tf_op jit(solution)/shard_map/ppermute | solution.py:16
  6.2 11.4 %collective-permute-start.1 = (f32[768,128]{1,0:T(8,128)S(1)}, f32[768,128]{1,0:T(8,128)S(1)}, u32[]{:S(2)}, u32[]{:S(2)}) collective-permute-start(f32[768,128]{1,0:T(8,128)S(1)} %get-tuple-element.62), channel_id=1, source_target_pairs={{4,0},{8,4},{12,8},{16,12},{20,16},{24,20},{28,24},{0,28},{5,1},{9... | collective-permute-start | bytes 1179656 | tf_op jit(solution)/shard_map/ppermute | solution.py:17
  9.3 8.3 %slice-start.4 = ((f32[2,12,96,512]{3,2,1,0:T(8,128)}), f32[2,12,32,512]{3,2,1,0:T(8,128)S(1)}, s32[]{:S(2)}) async-start(f32[2,12,96,512]{3,2,1,0:T(8,128)} %copy-done.1), calls=%async_computation.4 | async-start | bytes 3145728 | tf_op jit(solution)/shard_map/slice | solution.py:100
  16.1 4.8 %slice-start = ((s8[6291456]{0:T(1024)(128)(4,1)}), s8[4194304]{0:T(1024)(128)(4,1)S(1)}, s32[]{:S(2)}) async-start(s8[6291456]{0:T(1024)(128)(4,1)} %bitcast.80), calls=%async_computation | async-start | bytes 8388608
  17.7 3.2 %slice-start.1 = ((s8[6291456]{0:T(1024)(128)(4,1)}), s8[2097152]{0:T(1024)(128)(4,1)S(1)}, s32[]{:S(2)}) async-start(s8[6291456]{0:T(1024)(128)(4,1)} %bitcast.80), calls=%async_computation.1 | async-start | bytes 4194304
  18.9 1.9 %copy-start.3 = (bf16[256,32]{0,1:T(8,128)(2,1)S(1)}, bf16[256,32]{0,1:T(8,128)(2,1)}, u32[]{:S(2)}) copy-start(bf16[256,32]{0,1:T(8,128)(2,1)} %param.24) | copy-start | bytes 49156
  19.0 3.0 %copy-start.2 = (bf16[2,12,32,512]{3,2,1,0:T(8,128)(2,1)S(1)}, bf16[2,12,32,512]{3,2,1,0:T(8,128)(2,1)}, u32[]{:S(2)}) copy-start(bf16[2,12,32,512]{3,2,1,0:T(8,128)(2,1)} %param.18) | copy-start | bytes 2359300
  19.0 4.9 %copy-start.4 = (bf16[64,64]{1,0:T(8,128)(2,1)S(1)}, bf16[64,64]{1,0:T(8,128)(2,1)}, u32[]{:S(2)}) copy-start(bf16[64,64]{1,0:T(8,128)(2,1)} %param.21) | copy-start | bytes 24580
  19.0 4.9 %copy-start.6 = (f32[64]{0:T(128)S(1)}, f32[64]{0:T(128)}, u32[]{:S(2)}) copy-start(f32[64]{0:T(128)} %param.22) | copy-start | bytes 772
  19.0 9.4 %collective-permute-start.2 = (f32[768,128]{1,0:T(8,128)S(1)}, f32[768,128]{1,0:T(8,128)S(1)}, u32[]{:S(2)}, u32[]{:S(2)}) collective-permute-start(f32[768,128]{1,0:T(8,128)S(1)} %get-tuple-element.61), channel_id=1, source_target_pairs={{0,4},{4,8},{8,12},{12,16},{16,20},{20,24},{24,28},{28,0},{1,5},{5... | collective-permute-start | bytes 1179656 | tf_op jit(solution)/shard_map/ppermute | solution.py:16
  22.0 8.4 %slice-start.2 = ((s8[4718592]{0:T(1024)(128)(4,1)}), s8[4194304]{0:T(1024)(128)(4,1)S(1)}, s32[]{:S(2)}) async-start(s8[4718592]{0:T(1024)(128)(4,1)} %bitcast.82), calls=%async_computation.2 | async-start | bytes 8388608
  22.1 8.3 %slice-start.3 = ((s8[4718592]{0:T(1024)(128)(4,1)}), s8[524288]{0:T(1024)(128)(4,1)S(1)}, s32[]{:S(2)}) async-start(s8[4718592]{0:T(1024)(128)(4,1)} %bitcast.82), calls=%async_computation.3 | async-start | bytes 1048576
  22.1 8.2 %collective-permute-start.3 = (f32[768,128]{1,0:T(8,128)S(1)}, f32[768,128]{1,0:T(8,128)S(1)}, u32[]{:S(2)}, u32[]{:S(2)}) collective-permute-start(f32[768,128]{1,0:T(8,128)S(1)} %get-tuple-element.60), channel_id=1, source_target_pairs={{4,0},{8,4},{12,8},{16,12},{20,16},{24,20},{28,24},{0,28},{5,1},{9... | collective-permute-start | bytes 1179656 | tf_op jit(solution)/shard_map/ppermute | solution.py:17
  34.8 7.7 %collective-permute-start.4 = (bf16[768,128]{1,0:T(8,128)(2,1)S(1)}, bf16[768,128]{1,0:T(8,128)(2,1)S(1)}, u32[]{:S(2)}, u32[]{:S(2)}) collective-permute-start(bf16[768,128]{1,0:T(8,128)(2,1)S(1)} %get-tuple-element.66), channel_id=1, source_target_pairs={{0,4},{4,8},{8,12},{12,16},{16,20},{20,24},{24,28},{28,0},{1,5},{5... | collective-permute-start | bytes 589832 | tf_op jit(solution)/shard_map/ppermute | solution.py:16
  37.8 4.7 %collective-permute-start.5 = (bf16[768,128]{1,0:T(8,128)(2,1)S(1)}, bf16[768,128]{1,0:T(8,128)(2,1)S(1)}, u32[]{:S(2)}, u32[]{:S(2)}) collective-permute-start(bf16[768,128]{1,0:T(8,128)(2,1)S(1)} %get-tuple-element.67), channel_id=1, source_target_pairs={{4,0},{8,4},{12,8},{16,12},{20,16},{24,20},{28,24},{0,28},{5,1},{9... | collective-permute-start | bytes 589832 | tf_op jit(solution)/shard_map/ppermute | solution.py:17
  43.3 7.5 %collective-permute-start.6 = (bf16[768,128]{1,0:T(8,128)(2,1)S(1)}, bf16[768,128]{1,0:T(8,128)(2,1)S(1)}, u32[]{:S(2)}, u32[]{:S(2)}) collective-permute-start(bf16[768,128]{1,0:T(8,128)(2,1)S(1)} %get-tuple-element.64), channel_id=1, source_target_pairs={{0,4},{4,8},{8,12},{12,16},{16,20},{20,24},{24,28},{28,0},{1,5},{5... | collective-permute-start | bytes 589832 | tf_op jit(solution)/shard_map/ppermute | solution.py:16
  45.5 5.4 %collective-permute-start.7 = (bf16[768,128]{1,0:T(8,128)(2,1)S(1)}, bf16[768,128]{1,0:T(8,128)(2,1)S(1)}, u32[]{:S(2)}, u32[]{:S(2)}) collective-permute-start(bf16[768,128]{1,0:T(8,128)(2,1)S(1)} %get-tuple-element.65), channel_id=1, source_target_pairs={{4,0},{8,4},{12,8},{16,12},{20,16},{24,20},{28,24},{0,28},{5,1},{9... | collective-permute-start | bytes 589832 | tf_op jit(solution)/shard_map/ppermute | solution.py:17
where the time goes:
time: 96 us; the launch traced here: 95.7 us
  blocking collectives  43.2 us (45%)
  waiting for transfers between devices  19.6 us (20%)
  starting transfers between devices  12.7 us (13%)
  matrix products  11.4 us (12%)
  other arithmetic  6.26 us (7%)
  local copies, waits for them, and re-layouts  1.58 us (2%)
  between operations  0.96 us (1%)
    psum x1, blocking collectives, shards(): lax.psum((grad_conv, grad_bias, grad_mix, skip_weight_gradient), ('site',...  43.2 us
    ppermute x4, waiting for transfers between devices, with_halo(): before = lax.ppermute(last, axis, up)  17.7 us
    ppermute x4, starting transfers between devices, with_halo(): before = lax.ppermute(last, axis, up)  7.42 us
    ppermute x4, starting transfers between devices, with_halo(): after = lax.ppermute(first, axis, down)  5.33 us
  transfers between devices with their start and end apart: 8, of which 6 were waited for; matrix products, arithmetic and copies ran while one was open for 6% of the time, Pallas kernels for 0%

commit v1 on v0

v1 whole, which is shorter than its diff:
```python
import functools

import jax
import jax.numpy as jnp
from jax import lax
from jax.experimental import pallas as pl
from jax.experimental.pallas import tpu as pltpu
from jax.sharding import PartitionSpec as P

BLK = 128
GROUP = 8
MESH = pl.DeviceIdType.MESH
F32 = jnp.float32
BF16 = jnp.bfloat16


def mm(a, b):
    return jnp.dot(a, b, preferred_element_type=F32)


def nt(a, b):
    return lax.dot_general(a, b, (((1,), (1,)), ((), ())), preferred_element_type=F32)


def loop(n, f):
    def step(i, carry):
        f(i)
        return carry

    lax.fori_loop(0, n, step, 0)


def kernel(
    cfg,
    x_ref, co_ref, cs_ref, wc_ref, bias_ref, wm_ref, ws_ref, cols_ref, cnt_ref, adj_ref,
    out_conv, out_bias, out_mix, out_skip, out_gi,
    xm, xh, co, cs, av, a_mid, a_bnd, wct, wmt, wst, bcol,
    g2, c1, send_c, recv_c, fb, sg, mx, hh, f1h, gh, gp, gi,
    gs_acc, gm_acc, gc_acc, gb_acc, pack, rs_buf, dp_buf, fin,
    sem_loc, sem_cs, sem_out, e_send, e_recv, r_send, r_recv, d_send, d_recv, a_send, a_recv,
):
    n_site, n_dp, n_b, n_t, C, S, K, ct = cfg
    per_b = n_t // ct
    n_ch = n_b * per_b
    rows = ct * C
    nb = S // BLK
    site = lax.axis_index("site")
    dp = lax.axis_index("dp")
    right = lax.rem(site + 1, n_site)
    left = lax.rem(site + n_site - 1, n_site)
    n_q = (n_site // GROUP) * n_dp
    base = (site // GROUP) * GROUP
    loc = lax.rem(site, GROUP)
    q = (site // GROUP) * n_dp + dp

    def group_peer(j):
        return base + lax.rem(loc + j, GROUP)

    def cross_peer(j):
        other = lax.rem(q + j, n_q)
        return {"site": (other // n_dp) * GROUP + loc, "dp": lax.rem(other, n_dp)}

    barrier = pltpu.get_barrier_semaphore()
    signals = 0
    if n_site > GROUP:
        for p in (left, right):
            pl.semaphore_signal(barrier, inc=1, device_id={"site": p}, device_id_type=MESH)
            signals += 1
    for j in range(1, GROUP):
        pl.semaphore_signal(barrier, inc=1, device_id={"site": group_peer(j)}, device_id_type=MESH)
        signals += 1
    for j in range(1, n_q):
        pl.semaphore_signal(barrier, inc=1, device_id=cross_peer(j), device_id_type=MESH)
        signals += 1

    ld_adj = pltpu.make_async_copy(adj_ref, av, sem_loc.at[0])
    ld_co = pltpu.make_async_copy(co_ref, co, sem_loc.at[1])
    ld_x = pltpu.make_async_copy(x_ref, xm.at[:, 1:], sem_loc.at[2])
    ld_adj.start()
    ld_co.start()
    ld_x.start()

    def ld_cs(ch):
        r = pl.ds(ch * ct, ct)
        return pltpu.make_async_copy(cs_ref.at[r], cs.at[r], sem_cs.at[ch])

    for ch in range(n_ch):
        ld_cs(ch).start()

    wct[...] = wc_ref[...].astype(F32).T.astype(BF16)
    wmt[...] = wm_ref[...].astype(F32).T.astype(BF16)
    wst[...] = ws_ref[...].astype(F32).T.astype(BF16)
    bcol[...] = jnp.broadcast_to(bias_ref[...], (BLK, 2 * C)).T
    for b in range(n_b):
        xm[b, 0] = jnp.zeros((C, S), BF16)
        xh[b, 0] = jnp.zeros((C, 2 * BLK), BF16)
        gp[b, n_t] = jnp.zeros((2 * C, S), BF16)

    pl.semaphore_wait(barrier, signals)

    def remote(src, dst, e, side, ch, target):
        return pltpu.make_async_remote_copy(
            src_ref=src, dst_ref=dst, send_sem=e_send.at[e, side, ch],
            recv_sem=e_recv.at[e, side, ch], device_id={"site": target}, device_id_type=MESH,
        )

    lo, hi = pl.ds(0, BLK), pl.ds(S - BLK, BLK)
    h_lo, h_hi = pl.ds(0, BLK), pl.ds(BLK, BLK)

    def ex_x(ch):
        b, t0 = ch // per_b, lax.rem(ch, per_b) * ct
        src = x_ref.at[b, pl.ds(t0, ct)]
        dst = xh.at[b, pl.ds(t0 + 1, ct)]
        return (
            remote(src.at[:, :, hi], dst.at[:, :, h_lo], 0, 0, ch, right),
            remote(src.at[:, :, lo], dst.at[:, :, h_hi], 0, 1, ch, left),
        )

    def ex_c(which):
        def make(ch):
            r = pl.ds(ch * ct, ct)
            return (
                remote(send_c.at[which, 1, r], recv_c.at[which, 0, r], 1 + which, 0, ch, right),
                remote(send_c.at[which, 0, r], recv_c.at[which, 1, r], 1 + which, 1, ch, left),
            )

        return make

    def ex_f(ch):
        r = pl.ds(ch * ct, ct)
        src = mx.at[r, pl.ds(C, C)]
        dst = f1h.at[r]
        return (
            remote(src.at[:, :, hi], dst.at[:, :, h_lo], 3, 0, ch, right),
            remote(src.at[:, :, lo], dst.at[:, :, h_hi], 3, 1, ch, left),
        )

    def start(pair):
        for p in pair:
            p.start()

    def arrived(pair):
        for p in pair:
            p.wait_recv()

    for ch in range(n_ch):
        start(ex_x(ch))

    ld_adj.wait()
    for c in range(nb + 2):
        for r in range(nb):
            acc = jnp.zeros((BLK, BLK), F32)
            for k in range(K):
                on = jnp.where(
                    jnp.logical_and(cols_ref[r, k] == c, k < cnt_ref[r]), F32(1.0), F32(0.0)
                )
                acc = acc + av[r, k].astype(F32) * on
            blk = acc.astype(BF16)
            if c == 0 or c == nb + 1:
                o = 0 if c == 0 else BLK
                a_bnd[o : o + BLK, r * BLK : (r + 1) * BLK] = blk
            else:
                a_mid[(c - 1) * BLK : c * BLK, r * BLK : (r + 1) * BLK] = blk

    ld_co.wait()

    def back_one(ch):
        r = pl.ds(ch * ct, ct)
        for u in range(ct):
            t = ch * ct + u
            bm = mm(wmt[C:, :], co[t])
            c1[t] = bm[:C]
            g2[t] = bm[C:].astype(BF16)
        g = g2[r].reshape(rows, S)
        edge = nt(g, a_bnd[...]).astype(BF16).reshape(ct, C, 2 * BLK)
        send_c[0, 0, r] = edge[:, :, :BLK]
        send_c[0, 1, r] = edge[:, :, BLK:]
        start(ex_c(0)(ch))
        c1[r] = c1[r] + nt(g, a_mid[...]).reshape(ct, C, S)

    loop(n_ch, back_one)

    ld_x.wait()

    def forward_one(ch):
        b, t0 = ch // per_b, lax.rem(ch, per_b) * ct
        r = pl.ds(ch * ct, ct)
        arrived(ex_x(ch))
        for u in range(ct):
            t = ch * ct + u
            for src, width in ((xm, S), (xh, 2 * BLK)):
                st = src[b, pl.ds(t0 + u, 2)].reshape(2 * C, width)
                pre = mm(wc_ref[...], st) + bcol[:, 0:1]
                f = jnp.tanh(pre[:C])
                s = 0.5 * jnp.tanh(0.5 * pre[C:]) + 0.5
                h = (f * s).astype(BF16)
                if src is xm:
                    fb[t] = f
                    sg[t] = s
                    mx[t, 0:C] = h
                else:
                    hh[t] = h
        a = mx[r, 0:C].reshape(rows, S)
        f1 = mm(a, a_mid[...]) + mm(hh[r].reshape(rows, 2 * BLK), a_bnd[...])
        mx[r, C : 2 * C] = f1.astype(BF16).reshape(ct, C, S)
        start(ex_f(ch))

    loop(n_ch, forward_one)

    def back_two(ch):
        r = pl.ds(ch * ct, ct)
        arrived(ex_c(0)(ch))
        c1[r, :, lo] = c1[r, :, lo] + recv_c[0, 0, r].astype(F32)
        c1[r, :, hi] = c1[r, :, hi] + recv_c[0, 1, r].astype(F32)
        g = c1[r].astype(BF16).reshape(rows, S)
        edge = nt(g, a_bnd[...]).astype(BF16).reshape(ct, C, 2 * BLK)
        send_c[1, 0, r] = edge[:, :, :BLK]
        send_c[1, 1, r] = edge[:, :, BLK:]
        start(ex_c(1)(ch))
        gh[r] = nt(g, a_mid[...]).reshape(ct, C, S)

    loop(n_ch, back_two)

    gs_acc[...] = jnp.zeros_like(gs_acc)
    gm_acc[...] = jnp.zeros_like(gm_acc)
    gc_acc[...] = jnp.zeros_like(gc_acc)
    gb_acc[...] = jnp.zeros_like(gb_acc)

    def skip(ch):
        ld_cs(ch).wait()
        tot = gs_acc[...]
        for u in range(ct):
            t = ch * ct + u
            tot = tot + nt(mx[t, 0:C], cs[t])
            gh[t] = gh[t] + mm(wst[...], cs[t]) + mm(wmt[:C, :], co[t])
        gs_acc[...] = tot

    loop(n_ch, skip)

    def forward_two(ch):
        r = pl.ds(ch * ct, ct)
        arrived(ex_f(ch))
        f1 = mx[r, C : 2 * C].reshape(rows, S)
        f2 = mm(f1, a_mid[...]) + mm(f1h[r].reshape(rows, 2 * BLK), a_bnd[...])
        mx[r, 2 * C :] = f2.astype(BF16).reshape(ct, C, S)
        tot = gm_acc[:, : 3 * C]
        for u in range(ct):
            t = ch * ct + u
            tot = tot + nt(co[t], mx[t])
        gm_acc[:, : 3 * C] = tot

    loop(n_ch, forward_two)

    def finish(ch):
        b, t0 = ch // per_b, lax.rem(ch, per_b) * ct
        r = pl.ds(ch * ct, ct)
        arrived(ex_c(1)(ch))
        gh[r, :, lo] = gh[r, :, lo] + recv_c[1, 0, r].astype(F32)
        gh[r, :, hi] = gh[r, :, hi] + recv_c[1, 1, r].astype(F32)
        tot = gc_acc[:, : 2 * C]
        tob = gb_acc[...]
        for u in range(ct):
            t = ch * ct + u
            g, f, s = gh[t], fb[t], sg[t]
            gs = g * s
            v = jnp.concatenate([gs * (1.0 - f * f), gs * f * (1.0 - s)], axis=0).astype(BF16)
            gp[b, t0 + u] = v
            w = v.astype(F32)
            for m in range(nb):
                tob = tob + w[:, m * BLK : (m + 1) * BLK]
            tot = tot + nt(v, xm[b, pl.ds(t0 + u, 2)].reshape(2 * C, S))
        gc_acc[:, : 2 * C] = tot
        gb_acc[...] = tob

    loop(n_ch, finish)

    pack[:, 16:24, :] = jnp.zeros((GROUP, 8, BLK), F32)
    lane = lax.broadcasted_iota(jnp.int32, (2 * C, BLK), 1)
    both = jnp.where(lane < 2 * C, gc_acc[...], jnp.sum(gb_acc[...], axis=1, keepdims=True))
    for i in range(GROUP):
        o = 8 * (i % 4)
        p = BLK * (i // 4)
        pack[i, 0:8] = gs_acc[o : o + 8, p : p + BLK]
        pack[i, 8:16] = both[8 * i : 8 * i + 8]
        pack[i, 16:20] = gm_acc[4 * i : 4 * i + 4]

    def rs(j):
        peer = lax.rem(loc + j, GROUP)
        return pltpu.make_async_remote_copy(
            src_ref=pack.at[peer], dst_ref=rs_buf.at[j], send_sem=r_send.at[j],
            recv_sem=r_recv.at[j], device_id={"site": base + peer}, device_id_type=MESH,
        )

    def cross(j):
        return pltpu.make_async_remote_copy(
            src_ref=dp_buf.at[q], dst_ref=dp_buf.at[q], send_sem=d_send.at[j],
            recv_sem=d_recv.at[j], device_id=cross_peer(j), device_id_type=MESH,
        )

    def gather(j):
        return pltpu.make_async_remote_copy(
            src_ref=fin.at[loc], dst_ref=fin.at[loc], send_sem=a_send.at[j],
            recv_sem=a_recv.at[j], device_id={"site": group_peer(j)}, device_id_type=MESH,
        )

    for j in range(1, GROUP):
        rs(j).start()

    wct_now, wct_old = wct[C:, :], wct[:C, :]

    def inputs_grad(ch):
        b, t0 = ch // per_b, lax.rem(ch, per_b) * ct
        r = pl.ds(ch * ct, ct)
        for u in range(ct):
            v = mm(wct_now, gp[b, t0 + u]) + mm(wct_old, gp[b, t0 + u + 1])
            gi[ch * ct + u] = v.astype(BF16)
        pltpu.make_async_copy(gi.at[r], out_gi.at[b, pl.ds(t0, ct)], sem_out.at[ch]).start()

    loop(n_ch, inputs_grad)

    total = pack[loc]
    for j in range(1, GROUP):
        rs(j).wait_recv()
        total = total + rs_buf[j]
    dp_buf[q] = total
    for j in range(1, n_q):
        cross(j).start()
    for j in range(1, n_q):
        cross(j).wait_recv()
    total = dp_buf[0]
    for i in range(1, n_q):
        total = total + dp_buf[i]
    fin[loc] = total
    for j in range(1, GROUP):
        gather(j).start()
    for j in range(1, GROUP):
        gather(j).wait_recv()

    for h in range(2):
        out_skip[h * BLK : (h + 1) * BLK, :] = fin[4 * h : 4 * h + 4, 0:8].reshape(C, BLK).T
    both = fin[:, 8:16].reshape(2 * C, BLK)
    out_conv[...] = both[:, : 2 * C]
    out_bias[...] = both.T[2 * C : 2 * C + 1, :]
    for i in range(GROUP):
        out_mix[4 * i : 4 * i + 4, :] = fin[i, 16:20, : 3 * C]

    for ch in range(n_ch):
        for make in (ex_x, ex_c(0), ex_c(1), ex_f):
            for p in make(ch):
                p.wait_send()
        b, t0 = ch // per_b, (ch % per_b) * ct
        pltpu.make_async_copy(
            gi.at[pl.ds(ch * ct, ct)], out_gi.at[b, pl.ds(t0, ct)], sem_out.at[ch]
        ).wait()
    for j in range(1, GROUP):
        rs(j).wait_send()
        gather(j).wait_send()
    for j in range(1, n_q):
        cross(j).wait_send()


def shards(mesh_shape, x, co, cs, wc, bias, wm, ws, cols, cnt, adj):
    n_site, n_dp = mesh_shape
    n_b, n_t, C, S = x.shape
    K = cols.shape[1]
    skip = cs.shape[2]
    ct = 6
    n_ch = n_b * n_t // ct
    n = n_b * n_t
    n_q = (n_site // GROUP) * n_dp
    cfg = (n_site, n_dp, n_b, n_t, C, S, K, ct)
    vm = pl.BlockSpec(memory_space=pltpu.VMEM)
    sm = pl.BlockSpec(memory_space=pltpu.SMEM)
    anys = pl.BlockSpec(memory_space=pl.ANY)
    V = pltpu.VMEM
    D = pltpu.SemaphoreType.DMA
    scratch = [
        V((n_b, n_t + 1, C, S), BF16),
        V((n_b, n_t + 1, C, 2 * BLK), BF16),
        V((n, C, S), BF16),
        V((n, skip, S), BF16),
        V(adj.shape, BF16),
        V((S, S), BF16),
        V((2 * BLK, S), BF16),
        V((2 * C, 2 * C), BF16),
        V((3 * C, C), BF16),
        V((C, skip), BF16),
        V((2 * C, BLK), F32),
        V((n, C, S), BF16),
        V((n, C, S), F32),
        V((2, 2, n, C, BLK), BF16),
        V((2, 2, n, C, BLK), BF16),
        V((n, C, S), F32),
        V((n, C, S), F32),
        V((n, 3 * C, S), BF16),
        V((n, C, 2 * BLK), BF16),
        V((n, C, 2 * BLK), BF16),
        V((n, C, S), F32),
        V((n_b, n_t + 1, 2 * C, S), BF16),
        V((n, C, S), BF16),
        V((C, skip), F32),
        V((C, BLK), F32),
        V((2 * C, BLK), F32),
        V((2 * C, BLK), F32),
        V((GROUP, 24, BLK), F32),
        V((GROUP, 24, BLK), F32),
        V((n_q, 24, BLK), F32),
        V((GROUP, 24, BLK), F32),
        D((3,)),
        D((n_ch,)),
        D((n_ch,)),
        D((4, 2, n_ch)),
        D((4, 2, n_ch)),
        D((GROUP,)),
        D((GROUP,)),
        D((n_q,)),
        D((n_q,)),
        D((GROUP,)),
        D((GROUP,)),
    ]
    conv, gb, mix, gskip, gin = pl.pallas_call(
        functools.partial(kernel, cfg),
        out_shape=(
            jax.ShapeDtypeStruct((2 * C, 2 * C), F32),
            jax.ShapeDtypeStruct((1, 2 * C), F32),
            jax.ShapeDtypeStruct((C, 3 * C), F32),
            jax.ShapeDtypeStruct((skip, C), F32),
            jax.ShapeDtypeStruct(x.shape, BF16),
        ),
        in_specs=[anys, anys, anys, vm, vm, vm, vm, sm, sm, anys],
        out_specs=(vm, vm, vm, vm, anys),
        scratch_shapes=scratch,
        compiler_params=pltpu.CompilerParams(
            collective_id=0, has_side_effects=True, vmem_limit_bytes=60 * 1024 * 1024
        ),
        name="layer",
    )(x, co.reshape(n, C, S), cs.reshape(n, skip, S), wc, bias.reshape(1, -1), wm, ws, cols, cnt, adj)
    return conv, gb.reshape(-1), mix, gskip, gin


def solution(mesh):
    placed = (
        P("dp", None, None, "site"),
        P("dp", None, None, "site"),
        P("dp", None, None, "site"),
        P(),
        P(),
        P(),
        P(),
        P("site", None),
        P("site"),
        P("site", None, None, None),
    )
    return jax.shard_map(
        functools.partial(shards, (mesh.shape["site"], mesh.shape["dp"])),
        mesh=mesh,
        in_specs=placed,
        out_specs=(P(), P(), P(), P(), P("dp", None, None, "site")),
        check_vma=False,
    )
```

time: 96 us -> 47.6 us (0.50)
  blocking collectives: 43.2 us -> 0 us
  Pallas kernels: 0 us -> 37.6 us
  waiting for transfers between devices: 19.6 us -> 0 us
  starting transfers between devices: 12.7 us -> 0 us
  matrix products: 11.4 us -> 0 us
  local copies, waits for them, and re-layouts: 1.58 us -> 9 us
  other arithmetic: 6.26 us -> 0 us
    psum x1 -> x0, blocking collectives: 43.2 us -> none  [shards(): lax.psum((grad_conv, grad_bias, grad_mix, skip_weight_gradient), ('site',...]
    pallas_call x0 -> x1, Pallas kernels: none -> 37.6 us  [shards(): pl.pallas_call(functools.partial(kernel, cfg), out_shape=(jax.ShapeDtypeS...]
    ppermute x8 -> x0, waiting for transfers between devices: 19.6 us -> none  [the longest x4 17.7 us: with_halo(): before = lax.ppermute(last, axis, up)]
    ppermute x8 -> x0, starting transfers between devices: 12.7 us -> none  [the longest x4 7.42 us: with_halo(): before = lax.ppermute(last, axis, up)]
    dot_general x12 -> x0, matrix products: 11.4 us -> none  [the longest x1 1.91 us: shards(): jnp.einsum('btks,btcs->kc', cot_skip, hidden_state, preferred_element_typ...]
    unnamed x22 -> x6, local copies, waits for them, and re-layouts: 0.07 us -> 9 us
    another operation x2 -> x0, other arithmetic: 1.88 us -> none
    scatter-add x4 -> x0, other arithmetic: 1.75 us -> none  [the longest x2 1.55 us: hop_backward(): middle = middle.at[:, :BLK].add(received[:, :BLK])]
  transfers between devices with their start and end apart: 8 -> 0, of which waited for: 6 -> 0; matrix products, arithmetic and copies ran while one was open for 6% -> 0% of each run, Pallas kernels for 0% -> 0%
where the time goes in v1:
time: 47.6 us; the launch traced here: 47.2 us
  Pallas kernels  37.6 us (79%)
  local copies, waits for them, and re-layouts  9 us (19%)
  between operations  0.64 us (1%)
    pallas_call x1, Pallas kernels, shards(): pl.pallas_call(functools.partial(kernel, cfg), out_shape=(jax.ShapeDtypeS...  37.6 us
    unnamed x6, local copies, waits for them, and re-layouts  9 us

profile of v1, /device:TPU:0, one launch (start us, length us, event | category | flops | bytes accessed | tf_op | source)
XLA Modules:
  0.0 47.2 jit_solution(12233661401221803636)
XLA Ops:
  0.6 1.5 %copy.15.ws_ref = bf16[256,32]{1,0:T(8,128)(2,1)} copy(bf16[256,32]{0,1:T(8,128)(2,1)} %param.16) | data formatting | bytes 32768 | tf_op args[6]
  2.1 37.6 %layer.1 = (f32[64,64]{1,0:T(8,128)}, f32[1,64]{1,0:T(1,128)}, f32[32,96]{1,0:T(8,128)}, f32[256,32]{1,0:T(8,128)}, bf16[2,12,32,512]{3,2,1,0:T(8,128)(2,1)}) custom-call(bf16[2,12,32,512]{3,2,1,0:T(8,128)(2,1)} %x_ref.1, bf16[24,32,512]{2,1,0:T(8,128)(2,1)} %bitcast.5, bf16[24,256,512]{2,1,0:T(8,128)(2,1)} %bitcast.4, bf16[64,64]{1,0:T(8,128)(2,1)} %wc_ref.1, ...), custom_call_target="tpu_custom_call" | custom-call | tf_op jit(solution)/shard_map/layer/pallas_call | solution.py:421
  39.7 1.6 %copy.16 = f32[256,32]{0,1:T(8,128)} copy(f32[256,32]{1,0:T(8,128)} %get-tuple-element.18) | data formatting | bytes 65536
  41.3 1.4 %copy.21 = f32[64,64]{1,0:T(8,128)} copy(f32[64,64]{1,0:T(8,128)} %get-tuple-element.25) | data formatting | bytes 32768
  42.6 1.2 %copy.22 = f32[64]{0:T(128)} copy(f32[64]{0:T(128)} %bitcast.7) | data formatting | bytes 512
  43.8 1.3 %copy.23 = f32[32,96]{1,0:T(8,128)} copy(f32[32,96]{1,0:T(8,128)} %get-tuple-element.27) | data formatting | bytes 24576
  45.1 2.1 %copy.24 = bf16[2,12,32,512]{3,2,1,0:T(8,128)(2,1)} copy(bf16[2,12,32,512]{3,2,1,0:T(8,128)(2,1)} %get-tuple-element.29) | data formatting | bytes 1572864

commit v2 on v1

--- a/solution.py
+++ b/solution.py
@@ -9,6 +9,7 @@
 
 BLK = 128
 GROUP = 8
+VMEM_LIMIT = 40 * 1024 * 1024
 MESH = pl.DeviceIdType.MESH
 F32 = jnp.float32
 BF16 = jnp.bfloat16
@@ -32,12 +33,13 @@
 
 def kernel(
     cfg,
-    x_ref, co_ref, cs_ref, wc_ref, bias_ref, wm_ref, ws_ref, cols_ref, cnt_ref, adj_ref,
-    out_conv, out_bias, out_mix, out_skip, out_gi,
-    xm, xh, co, cs, av, a_mid, a_bnd, wct, wmt, wst, bcol,
-    g2, c1, send_c, recv_c, fb, sg, mx, hh, f1h, gh, gp, gi,
-    gs_acc, gm_acc, gc_acc, gb_acc, pack, rs_buf, dp_buf, fin,
-    sem_loc, sem_cs, sem_out, e_send, e_recv, r_send, r_recv, d_send, d_recv, a_send, a_recv,
+    x_ref, co_ref, cs_ref, wc_hbm, bias_hbm, wm_hbm, ws_hbm, cols_hbm, cnt_hbm, adj_ref,
+    fin, gi,
+    xm, xh, co, cs, av, a_mid, a_bnd, wct, wmt, bcol,
+    g2, c1, send_c, recv_c, fb, sg, mx, hh, f1h, gh, gp,
+    gs_acc, gm_acc, gc_acc, gb_acc, pack, rs_buf, dp_buf, got,
+    wc_ref, bias_ref, wm_ref, ws_ref, cols_ref, cnt_ref, sem_small,
+    sem_loc, sem_cs, e_send, e_recv, r_send, r_recv, d_send, d_recv, a_send, a_recv,
 ):
     n_site, n_dp, n_b, n_t, C, S, K, ct = cfg
     per_b = n_t // ct
@@ -73,6 +75,17 @@
         pl.semaphore_signal(barrier, inc=1, device_id=cross_peer(j), device_id_type=MESH)
         signals += 1
 
+    small = [
+        pltpu.make_async_copy(src, dst, sem_small.at[i])
+        for i, (src, dst) in enumerate(
+            (
+                (cols_hbm, cols_ref), (cnt_hbm, cnt_ref), (wm_hbm, wm_ref), (wc_hbm, wc_ref),
+                (bias_hbm, bias_ref), (ws_hbm, ws_ref),
+            )
+        )
+    ]
+    for cp in small:
+        cp.start()
     ld_adj = pltpu.make_async_copy(adj_ref, av, sem_loc.at[0])
     ld_co = pltpu.make_async_copy(co_ref, co, sem_loc.at[1])
     ld_x = pltpu.make_async_copy(x_ref, xm.at[:, 1:], sem_loc.at[2])
@@ -87,9 +100,10 @@
     for ch in range(n_ch):
         ld_cs(ch).start()
 
+    for cp in small:
+        cp.wait()
     wct[...] = wc_ref[...].astype(F32).T.astype(BF16)
     wmt[...] = wm_ref[...].astype(F32).T.astype(BF16)
-    wst[...] = ws_ref[...].astype(F32).T.astype(BF16)
     bcol[...] = jnp.broadcast_to(bias_ref[...], (BLK, 2 * C)).T
     for b in range(n_b):
         xm[b, 0] = jnp.zeros((C, S), BF16)
@@ -232,7 +246,7 @@
         for u in range(ct):
             t = ch * ct + u
             tot = tot + nt(mx[t, 0:C], cs[t])
-            gh[t] = gh[t] + mm(wst[...], cs[t]) + mm(wmt[:C, :], co[t])
+            gh[t] = gh[t] + mm(ws_ref[...], cs[t]) + mm(wmt[:C, :], co[t])
         gs_acc[...] = tot
 
     loop(n_ch, skip)
@@ -299,7 +313,7 @@
 
     def gather(j):
         return pltpu.make_async_remote_copy(
-            src_ref=fin.at[loc], dst_ref=fin.at[loc], send_sem=a_send.at[j],
+            src_ref=got.at[loc], dst_ref=got.at[loc], send_sem=a_send.at[j],
             recv_sem=a_recv.at[j], device_id={"site": group_peer(j)}, device_id_type=MESH,
         )
 
@@ -310,11 +324,9 @@
 
     def inputs_grad(ch):
         b, t0 = ch // per_b, lax.rem(ch, per_b) * ct
-        r = pl.ds(ch * ct, ct)
         for u in range(ct):
             v = mm(wct_now, gp[b, t0 + u]) + mm(wct_old, gp[b, t0 + u + 1])
-            gi[ch * ct + u] = v.astype(BF16)
-        pltpu.make_async_copy(gi.at[r], out_gi.at[b, pl.ds(t0, ct)], sem_out.at[ch]).start()
+            gi[b, t0 + u] = v.astype(BF16)
 
     loop(n_ch, inputs_grad)
 
@@ -330,33 +342,42 @@
     total = dp_buf[0]
     for i in range(1, n_q):
         total = total + dp_buf[i]
-    fin[loc] = total
+    got[loc] = total
     for j in range(1, GROUP):
         gather(j).start()
     for j in range(1, GROUP):
         gather(j).wait_recv()
 
-    for h in range(2):
-        out_skip[h * BLK : (h + 1) * BLK, :] = fin[4 * h : 4 * h + 4, 0:8].reshape(C, BLK).T
-    both = fin[:, 8:16].reshape(2 * C, BLK)
-    out_conv[...] = both[:, : 2 * C]
-    out_bias[...] = both.T[2 * C : 2 * C + 1, :]
-    for i in range(GROUP):
-        out_mix[4 * i : 4 * i + 4, :] = fin[i, 16:20, : 3 * C]
+    fin[...] = got[...]
 
     for ch in range(n_ch):
         for make in (ex_x, ex_c(0), ex_c(1), ex_f):
             for p in make(ch):
                 p.wait_send()
-        b, t0 = ch // per_b, (ch % per_b) * ct
-        pltpu.make_async_copy(
-            gi.at[pl.ds(ch * ct, ct)], out_gi.at[b, pl.ds(t0, ct)], sem_out.at[ch]
-        ).wait()
     for j in range(1, GROUP):
         rs(j).wait_send()
         gather(j).wait_send()
     for j in range(1, n_q):
         cross(j).wait_send()
+
+
+def unpack(fin, gi, out_conv, out_bias, out_mix, out_skip, out_gi, sem):
+    copy = pltpu.make_async_copy(gi, out_gi, sem)
+    copy.start()
+    n = out_conv.shape[0]
+    c = out_mix.shape[0]
+    for h in range(2):
+        out_skip[:, h * BLK : (h + 1) * BLK] = fin[4 * h : 4 * h + 4, 0:8].reshape(c, BLK)
+    both = fin[:, 8:16].reshape(n, BLK)
+    out_conv[...] = both[:, :n]
+    out_bias[...] = both.T[n : n + 1, :]
+    for i in range(GROUP):
+        out_mix[4 * i : 4 * i + 4, :] = fin[i, 16:20, : out_mix.shape[1]]
+    copy.wait()
+
+
+def pin(x):
+    return pltpu.with_memory_space_constraint(x, pltpu.HBM)
 
 
 def shards(mesh_shape, x, co, cs, wc, bias, wm, ws, cols, cnt, adj):
@@ -370,8 +391,7 @@
     n_q = (n_site // GROUP) * n_dp
     cfg = (n_site, n_dp, n_b, n_t, C, S, K, ct)
     vm = pl.BlockSpec(memory_space=pltpu.VMEM)
-    sm = pl.BlockSpec(memory_space=pltpu.SMEM)
-    anys = pl.BlockSpec(memory_space=pl.ANY)
+    anys = pl.BlockSpec(memory_space=pltpu.HBM)
     V = pltpu.VMEM
     D = pltpu.SemaphoreType.DMA
     scratch = [
@@ -384,7 +404,6 @@
         V((2 * BLK, S), BF16),
         V((2 * C, 2 * C), BF16),
         V((3 * C, C), BF16),
-        V((C, skip), BF16),
         V((2 * C, BLK), F32),
         V((n, C, S), BF16),
         V((n, C, S), F32),
@@ -397,7 +416,6 @@
         V((n, C, 2 * BLK), BF16),
         V((n, C, S), F32),
         V((n_b, n_t + 1, 2 * C, S), BF16),
-        V((n, C, S), BF16),
         V((C, skip), F32),
         V((C, BLK), F32),
         V((2 * C, BLK), F32),
@@ -406,8 +424,14 @@
         V((GROUP, 24, BLK), F32),
         V((n_q, 24, BLK), F32),
         V((GROUP, 24, BLK), F32),
+        V((2 * C, 2 * C), BF16),
+        V((1, 2 * C), F32),
+        V((C, 3 * C), BF16),
+        V((C, skip), BF16),
+        pltpu.SMEM(cols.shape, jnp.int32),
+        pltpu.SMEM(cnt.shape, jnp.int32),
+        D((6,)),
         D((3,)),
-        D((n_ch,)),
         D((n_ch,)),
         D((4, 2, n_ch)),
         D((4, 2, n_ch)),
@@ -418,24 +442,44 @@
         D((GROUP,)),
         D((GROUP,)),
     ]
+    fin, gi = pl.pallas_call(
+        functools.partial(kernel, cfg),
+        out_shape=(
+            jax.ShapeDtypeStruct((GROUP, 24, BLK), F32),
+            jax.ShapeDtypeStruct(x.shape, BF16),
+        ),
+        in_specs=[anys] * 10,
+        out_specs=(vm, vm),
+        scratch_shapes=scratch,
+        compiler_params=pltpu.CompilerParams(
+            collective_id=0, has_side_effects=True, vmem_limit_bytes=VMEM_LIMIT
+        ),
+        name="layer",
+    )(
+        *map(
+            pin,
+            (
+                x, co.reshape(n, C, S), cs.reshape(n, skip, S), wc, bias.reshape(1, -1), wm, ws.T,
+                cols, cnt, adj,
+            ),
+        )
+    )
     conv, gb, mix, gskip, gin = pl.pallas_call(
-        functools.partial(kernel, cfg),
+        unpack,
         out_shape=(
             jax.ShapeDtypeStruct((2 * C, 2 * C), F32),
             jax.ShapeDtypeStruct((1, 2 * C), F32),
             jax.ShapeDtypeStruct((C, 3 * C), F32),
-            jax.ShapeDtypeStruct((skip, C), F32),
+            jax.ShapeDtypeStruct((C, skip), F32),
             jax.ShapeDtypeStruct(x.shape, BF16),
         ),
-        in_specs=[anys, anys, anys, vm, vm, vm, vm, sm, sm, anys],
-        out_specs=(vm, vm, vm, vm, anys),
-        scratch_shapes=scratch,
-        compiler_params=pltpu.CompilerParams(
-            collective_id=0, has_side_effects=True, vmem_limit_bytes=60 * 1024 * 1024
-        ),
-        name="layer",
-    )(x, co.reshape(n, C, S), cs.reshape(n, skip, S), wc, bias.reshape(1, -1), wm, ws, cols, cnt, adj)
-    return conv, gb.reshape(-1), mix, gskip, gin
+        in_specs=[vm, vm],
+        out_specs=(vm, vm, vm, vm, pl.BlockSpec(memory_space=pltpu.HBM)),
+        scratch_shapes=[D],
+        compiler_params=pltpu.CompilerParams(vmem_limit_bytes=4 * 1024 * 1024),
+        name="results",
+    )(fin, gi)
+    return conv, gb.reshape(-1), mix, gskip.T, gin
 
 
 def solution(mesh):

time: 47.6 us -> 39.7 us (0.83)
  local copies, waits for them, and re-layouts: 9 us -> 0 us
  Pallas kernels: 37.6 us -> 38.9 us
    unnamed x6 -> x0, local copies, waits for them, and re-layouts: 9 us -> none
    pallas_call x0 -> x1, Pallas kernels: none -> 1.53 us  [shards(): pl.pallas_call(unpack, out_shape=(jax.ShapeDtypeStruct((2 * C, 2 * C), F3...]
where the time goes in v2:
time: 39.7 us; the launch traced here: 39.5 us
  Pallas kernels  38.9 us (98%)
  between operations  0.64 us (2%)
    pallas_call x1, Pallas kernels, shards(): pl.pallas_call(functools.partial(kernel, cfg), out_shape=(jax.ShapeDtypeS...  37.3 us
    pallas_call x1, Pallas kernels, shards(): pl.pallas_call(unpack, out_shape=(jax.ShapeDtypeStruct((2 * C, 2 * C), F3...  1.53 us

profile of v2, /device:TPU:0, one launch (start us, length us, event | category | flops | bytes accessed | tf_op | source)
XLA Modules:
  0.0 39.5 jit_solution(6587458321140202862)
XLA Ops:
  0.6 37.3 %layer.1 = (f32[8,24,128]{2,1,0:T(8,128)S(1)}, bf16[2,12,32,512]{3,2,1,0:T(8,128)(2,1)S(1)}) custom-call(bf16[2,12,32,512]{3,2,1,0:T(8,128)(2,1)} %x_ref.1, bf16[24,32,512]{2,1,0:T(8,128)(2,1)} %bitcast.7, bf16[24,256,512]{2,1,0:T(8,128)(2,1)} %bitcast.6, bf16[64,64]{1,0:T(8,128)(2,1)} %wc_hbm.1, f32[1,64]{1,0:T(1,128)} %bitcast.9, bf16[32,96]{1,0:T(8,128)(2,1)} %wm_hbm.1, ...), custom_call_target="tpu_custom_call" | custom-call | tf_op jit(solution)/shard_map/layer/pallas_call | solution.py:445
  38.0 1.5 %results.1 = (f32[64,64]{1,0:T(8,128)}, f32[1,64]{1,0:T(1,128)}, f32[32,96]{1,0:T(8,128)}, f32[32,256]{1,0:T(8,128)}, bf16[2,12,32,512]{3,2,1,0:T(8,128)(2,1)}) custom-call(f32[8,24,128]{2,1,0:T(8,128)S(1)} %get-tuple-element.12.fin, bf16[2,12,32,512]{3,2,1,0:T(8,128)(2,1)S(1)} %get-tuple-element.13.gi), custom_call_target="tpu_custom_call" | custom-call | tf_op jit(solution)/shard_map/results/pallas_call | solution.py:467

commit v3 on v2

--- a/solution.py
+++ b/solution.py
@@ -37,7 +37,8 @@
     fin, gi,
     xm, xh, co, cs, av, a_mid, a_bnd, wct, wmt, bcol,
     g2, c1, send_c, recv_c, fb, sg, mx, hh, f1h, gh, gp,
-    gs_acc, gm_acc, gc_acc, gb_acc, pack, rs_buf, dp_buf, got,
+    gs_acc, gm_acc, gc_acc, gb_acc,
+    pack_a, rs_a, dp_a, got_a, pack_b, rs_b, dp_b, got_b,
     wc_ref, bias_ref, wm_ref, ws_ref, cols_ref, cnt_ref, sem_small,
     sem_loc, sem_cs, e_send, e_recv, r_send, r_recv, d_send, d_recv, a_send, a_recv,
 ):
@@ -156,6 +157,57 @@
     def arrived(pair):
         for p in pair:
             p.wait_recv()
+
+    def sums(w, pack, rs_buf, dp_buf, got):
+        def rs(j):
+            peer = lax.rem(loc + j, GROUP)
+            return pltpu.make_async_remote_copy(
+                src_ref=pack.at[peer], dst_ref=rs_buf.at[j], send_sem=r_send.at[w, j],
+                recv_sem=r_recv.at[w, j], device_id={"site": base + peer}, device_id_type=MESH,
+            )
+
+        def cross(j):
+            return pltpu.make_async_remote_copy(
+                src_ref=dp_buf.at[q], dst_ref=dp_buf.at[q], send_sem=d_send.at[w, j],
+                recv_sem=d_recv.at[w, j], device_id=cross_peer(j), device_id_type=MESH,
+            )
+
+        def gather(j):
+            return pltpu.make_async_remote_copy(
+                src_ref=got.at[loc], dst_ref=got.at[loc], send_sem=a_send.at[w, j],
+                recv_sem=a_recv.at[w, j], device_id={"site": group_peer(j)}, device_id_type=MESH,
+            )
+
+        return rs, cross, gather, pack, rs_buf, dp_buf, got
+
+    def scatter(z):
+        for j in range(1, GROUP):
+            z[0](j).start()
+
+    def exchange(z):
+        rs, cross, gather, pack, rs_buf, dp_buf, got = z
+        total = pack[loc]
+        for j in range(1, GROUP):
+            rs(j).wait_recv()
+            total = total + rs_buf[j]
+        dp_buf[q] = total
+        for j in range(1, n_q):
+            cross(j).start()
+
+    def spread(z):
+        rs, cross, gather, pack, rs_buf, dp_buf, got = z
+        for j in range(1, n_q):
+            cross(j).wait_recv()
+        total = dp_buf[0]
+        for i in range(1, n_q):
+            total = total + dp_buf[i]
+        got[loc] = total
+        for j in range(1, GROUP):
+            gather(j).start()
+
+    def collect(z):
+        for j in range(1, GROUP):
+            z[2](j).wait_recv()
 
     for ch in range(n_ch):
         start(ex_x(ch))
@@ -265,6 +317,15 @@
 
     loop(n_ch, forward_two)
 
+    pack_a[:, 8:16, :] = jnp.zeros((GROUP, 8, BLK), F32)
+    for i in range(GROUP):
+        o = 8 * (i % 4)
+        p = BLK * (i // 4)
+        pack_a[i, 0:8] = gs_acc[o : o + 8, p : p + BLK]
+        pack_a[i, 8:12] = gm_acc[4 * i : 4 * i + 4]
+    early = sums(0, pack_a, rs_a, dp_a, got_a)
+    scatter(early)
+
     def finish(ch):
         b, t0 = ch // per_b, lax.rem(ch, per_b) * ct
         r = pl.ds(ch * ct, ct)
@@ -288,37 +349,13 @@
 
     loop(n_ch, finish)
 
-    pack[:, 16:24, :] = jnp.zeros((GROUP, 8, BLK), F32)
     lane = lax.broadcasted_iota(jnp.int32, (2 * C, BLK), 1)
     both = jnp.where(lane < 2 * C, gc_acc[...], jnp.sum(gb_acc[...], axis=1, keepdims=True))
     for i in range(GROUP):
-        o = 8 * (i % 4)
-        p = BLK * (i // 4)
-        pack[i, 0:8] = gs_acc[o : o + 8, p : p + BLK]
-        pack[i, 8:16] = both[8 * i : 8 * i + 8]
-        pack[i, 16:20] = gm_acc[4 * i : 4 * i + 4]
-
-    def rs(j):
-        peer = lax.rem(loc + j, GROUP)
-        return pltpu.make_async_remote_copy(
-            src_ref=pack.at[peer], dst_ref=rs_buf.at[j], send_sem=r_send.at[j],
-            recv_sem=r_recv.at[j], device_id={"site": base + peer}, device_id_type=MESH,
-        )
-
-    def cross(j):
-        return pltpu.make_async_remote_copy(
-            src_ref=dp_buf.at[q], dst_ref=dp_buf.at[q], send_sem=d_send.at[j],
-            recv_sem=d_recv.at[j], device_id=cross_peer(j), device_id_type=MESH,
-        )
-
-    def gather(j):
-        return pltpu.make_async_remote_copy(
-            src_ref=got.at[loc], dst_ref=got.at[loc], send_sem=a_send.at[j],
-            recv_sem=a_recv.at[j], device_id={"site": group_peer(j)}, device_id_type=MESH,
-        )
-
-    for j in range(1, GROUP):
-        rs(j).start()
+        pack_b[i] = both[8 * i : 8 * i + 8]
+    late = sums(1, pack_b, rs_b, dp_b, got_b)
+    scatter(late)
+    exchange(early)
 
     wct_now, wct_old = wct[C:, :], wct[:C, :]
 
@@ -330,35 +367,26 @@
 
     loop(n_ch, inputs_grad)
 
-    total = pack[loc]
-    for j in range(1, GROUP):
-        rs(j).wait_recv()
-        total = total + rs_buf[j]
-    dp_buf[q] = total
-    for j in range(1, n_q):
-        cross(j).start()
-    for j in range(1, n_q):
-        cross(j).wait_recv()
-    total = dp_buf[0]
-    for i in range(1, n_q):
-        total = total + dp_buf[i]
-    got[loc] = total
-    for j in range(1, GROUP):
-        gather(j).start()
-    for j in range(1, GROUP):
-        gather(j).wait_recv()
-
-    fin[...] = got[...]
+    exchange(late)
+    spread(early)
+    spread(late)
+    collect(early)
+    collect(late)
+
+    fin[:, 0:8, :] = got_a[:, 0:8, :]
+    fin[:, 8:16, :] = got_b[...]
+    fin[:, 16:24, :] = got_a[:, 8:16, :]
 
     for ch in range(n_ch):
         for make in (ex_x, ex_c(0), ex_c(1), ex_f):
             for p in make(ch):
                 p.wait_send()
-    for j in range(1, GROUP):
-        rs(j).wait_send()
-        gather(j).wait_send()
-    for j in range(1, n_q):
-        cross(j).wait_send()
+    for z in (early, late):
+        for j in range(1, GROUP):
+            z[0](j).wait_send()
+            z[2](j).wait_send()
+        for j in range(1, n_q):
+            z[1](j).wait_send()
 
 
 def unpack(fin, gi, out_conv, out_bias, out_mix, out_skip, out_gi, sem):
@@ -385,7 +413,7 @@
     n_b, n_t, C, S = x.shape
     K = cols.shape[1]
     skip = cs.shape[2]
-    ct = 6
+    ct = 12
     n_ch = n_b * n_t // ct
     n = n_b * n_t
     n_q = (n_site // GROUP) * n_dp
@@ -420,10 +448,14 @@
         V((C, BLK), F32),
         V((2 * C, BLK), F32),
         V((2 * C, BLK), F32),
-        V((GROUP, 24, BLK), F32),
-        V((GROUP, 24, BLK), F32),
-        V((n_q, 24, BLK), F32),
-        V((GROUP, 24, BLK), F32),
+        V((GROUP, 16, BLK), F32),
+        V((GROUP, 16, BLK), F32),
+        V((n_q, 16, BLK), F32),
+        V((GROUP, 16, BLK), F32),
+        V((GROUP, 8, BLK), F32),
+        V((GROUP, 8, BLK), F32),
+        V((n_q, 8, BLK), F32),
+        V((GROUP, 8, BLK), F32),
         V((2 * C, 2 * C), BF16),
         V((1, 2 * C), F32),
         V((C, 3 * C), BF16),
@@ -435,12 +467,12 @@
         D((n_ch,)),
         D((4, 2, n_ch)),
         D((4, 2, n_ch)),
-        D((GROUP,)),
-        D((GROUP,)),
-        D((n_q,)),
-        D((n_q,)),
-        D((GROUP,)),
-        D((GROUP,)),
+        D((2, GROUP)),
+        D((2, GROUP)),
+        D((2, n_q)),
+        D((2, n_q)),
+        D((2, GROUP)),
+        D((2, GROUP)),
     ]
     fin, gi = pl.pallas_call(
         functools.partial(kernel, cfg),

time: 39.7 us -> 38.6 us (0.972)
  Pallas kernels: 38.9 us -> 37.8 us
    pallas_call x1, Pallas kernels: 37.3 us -> 36.3 us  [shards(): pl.pallas_call(functools.partial(kernel, cfg), out_shape=(jax.ShapeDtypeS...]
where the time goes in v3:
time: 38.6 us; the launch traced here: 38.4 us
  Pallas kernels  37.8 us (98%)
  between operations  0.64 us (2%)
    pallas_call x1, Pallas kernels, shards(): pl.pallas_call(functools.partial(kernel, cfg), out_shape=(jax.ShapeDtypeS...  36.3 us
    pallas_call x1, Pallas kernels, shards(): pl.pallas_call(unpack, out_shape=(jax.ShapeDtypeStruct((2 * C, 2 * C), F3...  1.53 us

profile of v3, /device:TPU:0, one launch (start us, length us, event | category | flops | bytes accessed | tf_op | source)
XLA Modules:
  0.0 38.4 jit_solution(183210843301536248)
XLA Ops:
  0.6 36.3 %layer.1 = (f32[8,24,128]{2,1,0:T(8,128)S(1)}, bf16[2,12,32,512]{3,2,1,0:T(8,128)(2,1)S(1)}) custom-call(bf16[2,12,32,512]{3,2,1,0:T(8,128)(2,1)} %x_ref.1, bf16[24,32,512]{2,1,0:T(8,128)(2,1)} %bitcast.7, bf16[24,256,512]{2,1,0:T(8,128)(2,1)} %bitcast.6, bf16[64,64]{1,0:T(8,128)(2,1)} %wc_hbm.1, f32[1,64]{1,0:T(1,128)} %bitcast.9, bf16[32,96]{1,0:T(8,128)(2,1)} %wm_hbm.1, ...), custom_call_target="tpu_custom_call" | custom-call | tf_op jit(solution)/shard_map/layer/pallas_call | solution.py:477
  36.9 1.5 %results.1 = (f32[64,64]{1,0:T(8,128)}, f32[1,64]{1,0:T(1,128)}, f32[32,96]{1,0:T(8,128)}, f32[32,256]{1,0:T(8,128)}, bf16[2,12,32,512]{3,2,1,0:T(8,128)(2,1)}) custom-call(f32[8,24,128]{2,1,0:T(8,128)S(1)} %get-tuple-element.12.fin, bf16[2,12,32,512]{3,2,1,0:T(8,128)(2,1)S(1)} %get-tuple-element.13.gi), custom_call_target="tpu_custom_call" | custom-call | tf_op jit(solution)/shard_map/results/pallas_call | solution.py:499
